TPU v7x, 128 devices: a whole 4x4x4 slice. The times are simulated.
128 devices in a mesh: req: 64 (over z, y, x_hi, core), tp: 2 (over x_lo).
Axes of the slice: x: 4 (x_hi: 2, x_lo: 2; x = x_hi * 2 + x_lo), y: 4, z: 4, core: 2. Of those that a mesh axis runs over, the one named last changes fastest.
Arguments:
- arrivals: bfloat16 [32768, 2048], P('req', 'tp'), may hold values from -16 to 16
- packing: int32 [256], P('req'), may hold values from 0 to 255, as said below
- segment_ids: int32 [32768], P('req'), may hold values from 0 to 32767, as said below
- page_table: int32 [256], P('req'), may hold values from 0 to 255, as said below
- attn_gain: float32 [2048], replicated, may hold values from 0.25 to 1.75
- w_query: bfloat16 [2048, 2048], P(None, 'tp'), may hold values from -0.015625 to 0.015625
- w_key: bfloat16 [2048, 2048], P(None, 'tp'), may hold values from -0.125 to 0.125
- w_value: bfloat16 [2048, 2048], P(None, 'tp'), may hold values from -0.125 to 0.125
- w_out: bfloat16 [2048, 2048], P('tp'), may hold values from -0.1875 to 0.1875
- rel_bias: float32 [32, 32], P(None, 'tp'), may hold values from -4 to 260
- final_gain: float32 [2048], replicated, may hold values from 0.25 to 1.75
- cross_key: bfloat16 [2048, 2048], P(None, 'tp'), may hold values from -0.125 to 0.125
- cross_value: bfloat16 [2048, 2048], P(None, 'tp'), may hold values from -0.125 to 0.125
Outputs:
- hidden: bfloat16 [32768, 2048], P('req', 'tp')
- cache: bfloat16 [256, 128, 2, 2048], P('req', None, None, 'tp')
Inputs may be any that keep to these rules, and one draw needn't show every extreme that they name: `packing`: A permutation of the block numbers; the entries of index r of req name, by their quotient by 4, the indices r XOR m for every m below 4, each exactly 1 times. `segment_ids`: Non-decreasing; every segment lies within the 512 tokens of one index of req and has at most 256 tokens; some index holds one of exactly 256. `page_table`: A permutation of the slots; the entries of index r of req name, by their quotient by 4, the indices r XOR m for every m below 4, each exactly 1 times; slot s lies on index s // 4 of req.
All inputs are finite; a program needn't handle non-finite values.
Results may differ from a plain program's by a relative error of at most 0.01.
Values may be sent and summed in bfloat16 or wider, within the bound.
No kernel may reach another device: no remote copies, remote signals or barrier semaphores. Data moves between devices by JAX's collectives and lax.ppermute only.
A program may use at most 256 MiB of HBM per device.

v0:
```python
import jax
import jax.numpy as jnp
from jax import lax
from jax.sharding import PartitionSpec as P

PAGE = 128


epsilon = 1e-06
far_steps = (12, 16, 23, 32, 46, 64, 91)


def for_sending(value):
    return jax.tree.map(lambda a: a.astype(jnp.bfloat16) if a.dtype == jnp.float32 else a, value)


def swapped(block, axis, stride):
    count = lax.axis_size(axis)
    route = []
    for low in range(count):
        high = low | 1 << stride
        if high != low and high < count:
            route += [(low, high), (high, low)]
    return lax.ppermute(block, axis, route)


def buckets(offsets):
    distance = jnp.abs(offsets)
    far_bucket = 8 + sum(((distance >= threshold).astype(jnp.int32) for threshold in far_steps))
    bucket_ids = jnp.where(distance < 8, distance, far_bucket)
    return bucket_ids + jnp.where(offsets > 0, 16, 0).astype(jnp.int32)


def rms_scale(row_set, gain_row):
    values = row_set.astype(jnp.float32)
    mean_square = jnp.mean(values * values, axis=-1, keepdims=True)
    return (values * lax.rsqrt(mean_square + epsilon) * gain_row).astype(jnp.bfloat16)


def outgoing(row_set, targets, per_device, group_size, my_index):
    capacity = per_device // group_size
    owners = targets // per_device
    local_slot = targets % per_device
    lane_base = jnp.bitwise_xor(owners, my_index)
    position_index = jnp.arange(per_device, dtype=jnp.int32)
    same_owner = owners[:, None] == owners[None, :]
    earlier = position_index[None, :] < position_index[:, None]
    rank_index = jnp.sum((same_owner & earlier).astype(jnp.int32), axis=1)
    lane_index = lane_base * capacity + rank_index
    lane_ids = jnp.arange(per_device, dtype=jnp.int32)
    chosen = lane_index[None, :] == lane_ids[:, None]
    flat_rows = row_set.reshape(per_device, -1)
    buffer = jnp.dot(
        chosen.astype(row_set.dtype), flat_rows, preferred_element_type=jnp.float32
    ).astype(row_set.dtype)
    slot_tags = jnp.sum(jnp.where(chosen, local_slot[None, :] + 1, 0), axis=1) - 1
    return (
        buffer.reshape((group_size, capacity) + row_set.shape[1:]),
        slot_tags.reshape(group_size, capacity),
    )


def route(buffer, slot_tags, sections, sender):
    lane_count = buffer.shape[0]
    for bit_index in range(sections):
        outer_count = lane_count >> bit_index + 1
        inner_count = 1 << bit_index
        shaped_rows = buffer.reshape((outer_count, 2, inner_count) + buffer.shape[1:])
        shaped_tags = slot_tags.reshape(outer_count, 2, inner_count, slot_tags.shape[1])
        partner_rows, partner_tags = sender((shaped_rows[:, 1], shaped_tags[:, 1]), bit_index)
        buffer = jnp.stack([shaped_rows[:, 0], partner_rows], axis=1).reshape(buffer.shape)
        slot_tags = jnp.stack([shaped_tags[:, 0], partner_tags], axis=1).reshape(slot_tags.shape)
    return (buffer, slot_tags)


def incoming(received, slot_tags, per_device):
    flat_rows = received.reshape(slot_tags.size, -1)
    wanted = slot_tags.reshape(-1)[None, :] == jnp.arange(per_device, dtype=jnp.int32)[:, None]
    placed = jnp.dot(
        wanted.astype(received.dtype), flat_rows, preferred_element_type=jnp.float32
    ).astype(received.dtype)
    return placed.reshape((per_device,) + received.shape[2:])


def cross_pages(final_rows, cross_key, cross_value, block_count):
    cross_keys = jnp.dot(final_rows, cross_key, preferred_element_type=jnp.float32).astype(
        jnp.bfloat16
    )
    cross_values = jnp.dot(final_rows, cross_value, preferred_element_type=jnp.float32).astype(
        jnp.bfloat16
    )
    return jnp.stack([cross_keys, cross_values], axis=1).reshape(
        block_count, PAGE, 2, cross_key.shape[1]
    )


def offset_tile(rel_bias, first_row, row_block, token_count):
    span = token_count + row_block
    lane = jnp.arange(span, dtype=jnp.int32)
    offsets = jnp.where(lane < token_count, lane, lane - span) - first_row
    bucket_ids = buckets(offsets)
    selector = (
        bucket_ids[:, None] == jnp.arange(rel_bias.shape[0], dtype=jnp.int32)[None, :]
    ).astype(jnp.float32)
    bias_row = jnp.transpose(jnp.dot(selector, rel_bias, precision=lax.Precision.HIGHEST))
    head_count = bias_row.shape[0]
    repeated = jnp.tile(bias_row, (1, row_block))[:, : row_block * (span - 1)]
    return repeated.reshape(head_count, row_block, span - 1)[:, :, :token_count]


def attend(queries, keys_local, values_local, segments, rel_bias):
    token_count = queries.shape[0]
    head_count = rel_bias.shape[1]
    head_dim = queries.shape[1] // head_count
    row_block = min(512, token_count)
    query_heads = queries.reshape(token_count, head_count, head_dim)
    key_heads = keys_local.reshape(token_count, head_count, head_dim)
    value_heads = values_local.reshape(token_count, head_count, head_dim)

    def one_block(first_row):
        scores = jnp.einsum(
            "qhd,khd->hqk", query_heads, key_heads, preferred_element_type=jnp.float32
        )
        bias_tile = offset_tile(rel_bias, first_row, row_block, token_count)
        same_segment = segments[:, None] == segments[None, :]
        scores = jnp.where(same_segment[None], scores + bias_tile, -jnp.inf)
        row_max = jnp.max(scores, axis=-1, keepdims=True)
        weights = jnp.exp(scores - row_max)
        probabilities = (weights / jnp.sum(weights, axis=-1, keepdims=True)).astype(jnp.bfloat16)
        mixed = jnp.einsum(
            "hqk,khd->qhd", probabilities, value_heads, preferred_element_type=jnp.float32
        )
        return mixed.astype(jnp.bfloat16)

    block_starts = jnp.arange(token_count // row_block, dtype=jnp.int32) * row_block
    outcome = lax.map(one_block, block_starts)
    return outcome.reshape(token_count, head_count * head_dim)


def shards(
    arrivals,
    packing,
    segment_ids,
    page_table,
    attn_gain,
    w_query,
    w_key,
    w_value,
    w_out,
    rel_bias,
    final_gain,
    cross_key,
    cross_value,
):
    req_count = lax.axis_size("req")
    my_index = lax.axis_index("req")
    token_count, share_width = arrivals.shape
    block_count = token_count // PAGE
    group_size = min(block_count, req_count)
    sections = group_size.bit_length() - 1
    buffer, slot_tags = outgoing(
        arrivals.reshape(block_count, PAGE, share_width), packing, block_count, group_size, my_index
    )
    moved, moved_tags = route(
        buffer,
        slot_tags,
        sections,
        lambda pieces, bit_index: swapped((pieces[0], for_sending(pieces[1])), "req", bit_index),
    )
    packed = incoming(moved, moved_tags, block_count).reshape(token_count, share_width)
    whole = lax.all_gather(packed, "tp", axis=1, tiled=True)
    normed = rms_scale(whole, attn_gain)
    queries = jnp.dot(normed, w_query, preferred_element_type=jnp.float32).astype(jnp.bfloat16)
    keys_local = jnp.dot(normed, w_key, preferred_element_type=jnp.float32).astype(jnp.bfloat16)
    values_local = jnp.dot(normed, w_value, preferred_element_type=jnp.float32).astype(jnp.bfloat16)
    context = attend(queries, keys_local, values_local, segment_ids, rel_bias)
    product = jnp.dot(context, w_out, preferred_element_type=jnp.float32)
    column_start = lax.axis_index("tp") * share_width
    summed = lax.psum(product.astype(jnp.bfloat16), "tp").astype(jnp.float32)
    hidden_full = (whole.astype(jnp.float32) + summed).astype(jnp.bfloat16)
    final_full = rms_scale(hidden_full, final_gain)
    hidden_out = lax.dynamic_slice_in_dim(hidden_full, column_start, share_width, 1)
    pages = cross_pages(final_full, cross_key, cross_value, block_count)
    page_buffer, page_tags = outgoing(pages, page_table, block_count, group_size, my_index)
    routed, routed_tags = route(
        page_buffer,
        page_tags,
        sections,
        lambda pieces, bit_index: swapped((pieces[0], for_sending(pieces[1])), "req", bit_index),
    )
    cache = incoming(routed, routed_tags, block_count)
    return (hidden_out, cache)


def solution(mesh):
    return jax.shard_map(
        shards,
        mesh=mesh,
        in_specs=(
            P("req", "tp"),
            P("req"),
            P("req"),
            P("req"),
            P(),
            P(None, "tp"),
            P(None, "tp"),
            P(None, "tp"),
            P("tp", None),
            P(None, "tp"),
            P(),
            P(None, "tp"),
            P(None, "tp"),
        ),
        out_specs=(P("req", "tp"), P("req", None, None, "tp")),
        check_vma=False,
    )
```

profile of v0, /device:TPU:1, one launch (start us, length us, event | category | flops | bytes accessed | tf_op | source)
XLA Modules:
  0.0 407.6 jit_solution(4950677926563563998)
XLA Ops:
  7.2 2.0 reshape_reshape.36
  9.2 1.3 fusion.32
  13.1 1.5 collective-permute-start.2
  14.8 1.3 collective-permute-done.2
  16.3 2.9 collective-permute-start.3
  20.2 0.8 collective-permute-done
  21.3 9.8 %collective-permute-done.1 = s32[1,2,1]{1,2,0:T(1,128)S(1)} collective-permute-done((s32[1,2,1]{1,2,0:T(1,128)S(1)}, s32[1,2,1]{1,2,0:T(1,128)S(1)}, u32[]{:S(2)}, u32[]{:S(2)}) %collective-permute-start.1) | collective-permute-done | bytes 40 | tf_op jit(solution)/shard_map/ppermute | solution.py:24
  31.3 0.8 copy.62
  32.8 1.9 reshape_reshape.40
  35.5 4.4 %tile.14 = f32[16,512,1024]{2,1,0:T(8,128)S(1)} broadcast(f32[16,1024]{1,0:T(8,128)S(1)} %convolution_bitcast_fusion), dimensions={0,2} | broadcast | bytes 33619968 | tf_op jit(solution)/shard_map/while/body/eval_jaxpr/tile | solution.py:107
  39.9 39.7 %copy.63 = f32[2,8,512,1024]{3,1,2,0:T(8,128)} copy(f32[2,8,512,1024]{3,2,1,0:T(8,128)S(1)} %bitcast.87) | data formatting | bytes 67108864
  79.6 22.6 %slice.78 = f32[16,523776]{1,0:T(8,128)} slice(f32[16,524288]{1,0:T(8,128)} %bitcast.88), slice={[0:16], [0:523776]} | slice | bytes 67043328 | tf_op jit(solution)/shard_map/while/body/eval_jaxpr/slice | solution.py:107
  102.1 51.4 %reshape.149 = f32[16,512,1023]{2,1,0:T(8,128)} reshape(f32[16,523776]{1,0:T(8,128)} %slice.78) | data formatting | bytes 67043328 | tf_op jit(solution)/shard_map/while/body/eval_jaxpr/reshape | solution.py:108
  153.5 11.6 %slice.79 = f32[16,512,512]{2,1,0:T(8,128)} slice(f32[16,512,1023]{2,1,0:T(8,128)} %reshape.149), slice={[0:16], [0:512], [0:512]} | slice | bytes 33554432 | tf_op jit(solution)/shard_map/while/body/eval_jaxpr/slice | solution.py:108
  165.1 17.6 %copy.58 = f32[16,512,512]{1,2,0:T(8,128)} copy(f32[16,512,512]{2,1,0:T(8,128)} %slice.79) | data formatting | bytes 33554432
  183.0 2.1 fusion.5
  185.1 5.3 %convolution_convert_fusion.9 = bf16[512,1024]{1,0:T(8,128)(2,1)S(1)} fusion(bf16[2048,1024]{1,0:T(8,128)(2,1)} %param.20, bf16[512,2048]{1,0:T(8,128)(2,1)} %all-gather.2.cloned.1.call-done, f32[2048]{0:T(1024)S(1)} %copy-done.10, f32[512]{0:T(512)S(1)} %add_rsqrt_fusion.1), kind=kOutput, calls=%fused_computation.30 | convolution fusion | flops 2152202240 | bytes 7350272 | tf_op jit(solution)/shard_map/dot_general | solution.py:175
  190.4 1.3 copy.45
  191.8 5.6 %convolution_convert_fusion.8 = bf16[512,1024]{1,0:T(8,128)(2,1)} fusion(bf16[2048,1024]{1,0:T(8,128)(2,1)} %param.18, bf16[512,2048]{1,0:T(8,128)(2,1)S(1)} %copy-done.2, f32[2048]{0:T(1024)S(1)} %copy-done.10, f32[512]{0:T(512)S(1)} %add_rsqrt_fusion.1), kind=kOutput, calls=%fused_computation.29 | convolution fusion | flops 2152202240 | bytes 7350272 | tf_op jit(solution)/shard_map/dot_general | solution.py:173
  197.3 1.5 copy.46
  198.8 5.6 %convolution_convert_fusion.7 = bf16[512,1024]{1,0:T(8,128)(2,1)} fusion(bf16[2048,1024]{1,0:T(8,128)(2,1)} %param.19, bf16[512,2048]{1,0:T(8,128)(2,1)S(1)} %copy-done.2, f32[2048]{0:T(1024)S(1)} %copy-done.10, f32[512]{0:T(512)S(1)} %add_rsqrt_fusion.1), kind=kOutput, calls=%fused_computation.28 | convolution fusion | flops 2152202240 | bytes 7350272 | tf_op jit(solution)/shard_map/dot_general | solution.py:174
  204.4 2.3 copy.47
  206.7 14.3 %add_select_fusion = f32[16,512,512]{1,2,0:T(8,128)} fusion(f32[16,512,512]{1,2,0:T(8,128)} %copy.58, bf16[512,16,64]{0,2,1:T(8,128)(2,1)S(1)} %bitcast.91, bf16[512,16,64]{0,2,1:T(8,128)(2,1)} %bitcast.92, pred[512,512]{0,1:T(8,128)(4,1)S(1)} %broadcast_compare_fusion), kind=kOutput, calls=%fused_computation.7 | convolution fusion | flops 545259520 | bytes 35913728 | tf_op jit(solution)/shard_map/while/body/eval_jaxpr/qhd,khd->hqk/dot_general | solution.py:121
  221.0 12.1 %fusion.42 = f32[16,512]{1,0:T(8,128)S(1)} fusion(f32[16,512,512]{1,2,0:T(8,128)} %add_select_fusion), kind=kOutput, calls=%fused_computation.106 | output fusion | flops 8389119 | bytes 16809984 | tf_op jit(solution)/shard_map/while/body/eval_jaxpr/sub | solution.py:128
  233.1 13.8 %fusion.9 = bf16[16,64,512]{2,1,0:T(8,128)(2,1)} fusion(bf16[512,16,64]{0,2,1:T(8,128)(2,1)S(1)} %bitcast.95, f32[16,512]{1,0:T(8,128)S(1)} %fusion.42, f32[16,512,512]{1,2,0:T(8,128)} %add_select_fusion), kind=kOutput, calls=%fused_computation.25 | convolution fusion | flops 549986816 | bytes 18907136 | tf_op jit(solution)/shard_map/while/body/eval_jaxpr/hqk,khd->qhd/dot_general | solution.py:130
  246.9 6.2 %convolution_convert_fusion.4 = bf16[512,2048]{1,0:T(8,128)(2,1)} fusion(bf16[512,1024]{0,1:T(8,128)(2,1)} %bitcast.105, bf16[1024,2048]{1,0:T(8,128)(2,1)} %param.21), kind=kOutput, calls=%fused_computation.21 | convolution fusion | flops 2148532224 | bytes 7340032 | tf_op jit(solution)/shard_map/dot_general | solution.py:177
  253.1 72.7 %all-reduce.2.cloned.1.call-done = bf16[512,2048]{1,0:T(8,128)(2,1)} async-done(((bf16[512,2048]{1,0:T(8,128)(2,1)}), bf16[512,2048]{1,0:T(8,128)(2,1)}) %all-reduce.2.cloned.1.call-update) | async-done | bytes 2097168 | tf_op jit(solution)/shard_map/psum | solution.py:179
  325.8 2.7 fusion.2
  328.6 2.4 fusion.11
  331.5 2.4 fusion.10
  334.1 3.5 copy.52
  337.6 2.9 reshape_reshape.42
  340.6 2.6 convolution_convert_fusion.1
  343.1 4.1 %reshape_reshape.43 = bf16[2,2,1,1,128,2,1024]{6,5,4,1,0,3,2:T(2,128)(2,1)S(1)} reshape(bf16[4,262144]{1,0:T(4,128)(2,1)} %convolution_convert_fusion.1) | data formatting | bytes 4194304 | tf_op jit(solution)/shard_map/reshape;reshape | solution.py:68
  347.2 1.5 slice_bitcast_fusion.3
  348.7 0.8 collective-permute-start.6
  349.5 2.3 collective-permute-done.6
  351.8 3.0 maximum_bitcast_fusion
  354.7 2.3 slice_bitcast_fusion.1
  357.0 2.4 collective-permute-start.7
  360.5 0.8 collective-permute-done.4
  361.5 0.7 collective-permute-start.5
  362.3 20.9 %collective-permute-done.5 = s32[1,2,1]{1,2,0:T(1,128)S(1)} collective-permute-done((s32[1,2,1]{1,2,0:T(1,128)S(1)}, s32[1,2,1]{1,2,0:T(1,128)S(1)}, u32[]{:S(2)}, u32[]{:S(2)}) %collective-permute-start.5) | collective-permute-done | bytes 40 | tf_op jit(solution)/shard_map/ppermute | solution.py:24
  383.3 1.1 constant_dynamic-slice_fusion
  384.4 5.7 %pad_maximum_fusion.1 = bf16[1,2,2,1,128,2,1024]{6,5,4,2,3,1,0:T(2,128)(2,1)} fusion(bf16[1,1,2,1,128,2,1024]{6,5,4,2,3,1,0:T(2,128)(2,1)} %bitcast.27, bf16[1,1,2,1,128,2,1024]{6,5,4,2,3,1,0:T(2,128)(2,1)S(1)} %get-tuple-element.18), kind=kLoop, calls=%fused_computation.24 | loop fusion | flops 1048576 | bytes 4194304 | tf_op jit(solution)/shard_map/stack | solution.py:71
  390.0 2.9 reshape_reshape.45
  393.0 2.6 convolution_convert_fusion
  395.6 5.0 %reshape.151 = bf16[4,128,2,1024]{3,2,1,0:T(2,128)(2,1)} reshape(bf16[4,262144]{1,0:T(4,128)(2,1)} %convolution_convert_fusion) | data formatting | bytes 4194304 | tf_op jit(solution)/shard_map/reshape | solution.py:82
  (71 shorter events, 8.4 us)
Async XLA Ops:
  7.2 27.9 %copy-start = (f32[32,16]{0,1:T(8,128)S(1)}, f32[32,16]{0,1:T(8,128)}, u32[]{:S(2)}) copy-start(f32[32,16]{0,1:T(8,128)} %param.22) | copy-start | bytes 6148
  7.2 175.8 %all-gather.2.cloned.1.call-start = ((), (), s32[]{:S(2)}) async-start(), calls=%async_computation | async-start | bytes 3145728 | tf_op jit(solution)/shard_map/all_gather | solution.py:171
  13.1 3.0 collective-permute-start.2
  16.3 14.8 %collective-permute-start.3 = (bf16[1,2,1,128,1024]{4,3,1,2,0:T(8,128)(2,1)S(1)}, bf16[1,2,1,128,1024]{4,3,1,2,0:T(8,128)(2,1)S(1)}, u32[]{:S(2)}, u32[]{:S(2)}) collective-permute-start(bf16[1,2,1,128,1024]{4,3,1,2,0:T(8,128)(2,1)S(1)} %get-tuple-element.30), channel_id=1, source_target_pairs={{0,4},{4,0},{2,6},{6,2},{8,12},{12,8},{10,14},{14,10},{16,20},{20,... | collective-permute-start | bytes 1572872 | tf_op jit(solution)/shard_map/ppermute | solution.py:24
  19.4 1.5 collective-permute-start
  21.2 9.9 %collective-permute-start.1 = (s32[1,2,1]{1,2,0:T(1,128)S(1)}, s32[1,2,1]{1,2,0:T(1,128)S(1)}, u32[]{:S(2)}, u32[]{:S(2)}) collective-permute-start(s32[1,2,1]{1,2,0:T(1,128)S(1)} %get-tuple-element.38), channel_id=1, source_target_pairs={{0,4},{4,0},{2,6},{6,2},{8,12},{12,8},{10,14},{14,10},{16,20},{20,... | collective-permute-start | bytes 32 | tf_op jit(solution)/shard_map/ppermute | solution.py:24
  34.7 291.1 %all-reduce.2.cloned.1.call-start = ((), (), s32[]{:S(2)}) async-start(), calls=%async_computation.1 | async-start | bytes 4194304 | tf_op jit(solution)/shard_map/psum | solution.py:179
  165.1 17.6 %copy-start.6 = (s32[512]{0:T(512)S(1)}, s32[512]{0:T(512)}, u32[]{:S(2)}) copy-start(s32[512]{0:T(512)} %param.15) | copy-start | bytes 6148
  165.1 20.0 %copy-start.10 = (f32[2048]{0:T(1024)S(1)}, f32[2048]{0:T(1024)}, u32[]{:S(2)}) copy-start(f32[2048]{0:T(1024)} %param.17) | copy-start | bytes 24580
  185.1 6.7 %copy-start.2 = (bf16[512,2048]{1,0:T(8,128)(2,1)S(1)}, bf16[512,2048]{1,0:T(8,128)(2,1)}, u32[]{:S(2)}) copy-start(bf16[512,2048]{1,0:T(8,128)(2,1)} %all-gather.2.cloned.1.call-done) | copy-start | bytes 6291460
  221.0 12.1 %copy-start.5 = (bf16[512,1024]{0,1:T(8,128)(2,1)S(1)}, bf16[512,1024]{0,1:T(8,128)(2,1)}, u32[]{:S(2)}) copy-start(bf16[512,1024]{0,1:T(8,128)(2,1)} %copy.45) | copy-start | bytes 3145732
  253.1 75.5 %copy-start.11 = (f32[2048]{0:T(1024)S(1)}, f32[2048]{0:T(1024)}, u32[]{:S(2)}) copy-start(f32[2048]{0:T(1024)} %param.23) | copy-start | bytes 24580
  325.8 2.8 copy-start.8
  328.6 2.5 copy-start.3
  328.6 2.9 copy-start.9
  334.1 6.4 %copy-start.7 = (s32[4]{0:T(128)S(1)}, s32[4]{0:T(128)}, u32[]{:S(2)}) copy-start(s32[4]{0:T(128)} %get-tuple-element.45) | copy-start | bytes 52
  348.7 3.0 collective-permute-start.6
  351.8 7.6 %copy-start.12 = (s32[4]{0:T(128)S(1)}, s32[4]{0:T(128)}, u32[]{:S(2)}) copy-start(s32[4]{0:T(128)} %get-tuple-element.41) | copy-start | bytes 52
  351.8 31.5 %copy-start.4 = (bf16[512,2048]{1,0:T(8,128)(2,1)S(1)}, bf16[512,2048]{1,0:T(8,128)(2,1)}, u32[]{:S(2)}) copy-start(bf16[512,2048]{1,0:T(8,128)(2,1)} %copy-done.3) | copy-start | bytes 6291460
  357.0 27.4 %collective-permute-start.7 = (bf16[1,2,1,128,2,1024]{5,4,3,1,2,0:T(2,128)(2,1)}, bf16[1,2,1,128,2,1024]{5,4,3,1,2,0:T(2,128)(2,1)}, u32[]{:S(2)}, u32[]{:S(2)}) collective-permute-start(bf16[1,2,1,128,2,1024]{5,4,3,1,2,0:T(2,128)(2,1)} %get-tuple-element.19), channel_id=1, source_target_pairs={{0,4},{4,0},{2,6},{6,2},{8,12},{12,8},{10,14},{14,10},{16,20},{20,... | collective-permute-start | bytes 3145736 | tf_op jit(solution)/shard_map/ppermute | solution.py:24
  359.8 1.5 collective-permute-start.4
  361.5 21.7 %collective-permute-start.5 = (s32[1,2,1]{1,2,0:T(1,128)S(1)}, s32[1,2,1]{1,2,0:T(1,128)S(1)}, u32[]{:S(2)}, u32[]{:S(2)}) collective-permute-start(s32[1,2,1]{1,2,0:T(1,128)S(1)} %get-tuple-element.34), channel_id=1, source_target_pairs={{0,4},{4,0},{2,6},{6,2},{8,12},{12,8},{10,14},{14,10},{16,20},{20,... | collective-permute-start | bytes 32 | tf_op jit(solution)/shard_map/ppermute | solution.py:24
  390.0 10.5 %copy-start.1 = (f32[32,16]{0,1:T(8,128)S(1)}, f32[32,16]{0,1:T(8,128)}, u32[]{:S(2)}) copy-start(f32[32,16]{0,1:T(8,128)} %param.22) | copy-start | bytes 6148
Sparse Core Ops, SparseCore 0:
  34.8 38.6 all-gather.1
  253.3 72.5 all-reduce.1
where the time goes:
time: 413 us; the launch traced here: 408 us
  local copies, waits for them, and re-layouts  182 us (44%)
  waiting for transfers between devices  109 us (26%)
  matrix products  62.5 us (15%)
  other arithmetic  29.4 us (7%)
  between operations  14.5 us (4%)
  starting transfers between devices  10.3 us (2%)
    psum x1, waiting for transfers between devices, shards(): summed = lax.psum(product.astype(jnp.bfloat16), 'tp').astype(jnp.float32)  72.7 us
    unnamed x34, local copies, waits for them, and re-layouts  62.9 us
    reshape x1, local copies, waits for them, and re-layouts, offset_tile(): return repeated.reshape(head_count, row_block, span - 1)[:, :, :token_count]  51.4 us
    ppermute x8, waiting for transfers between devices, swapped(): return lax.ppermute(block, axis, route)  35.9 us
    slice x1, local copies, waits for them, and re-layouts, offset_tile(): repeated = jnp.tile(bias_row, (1, row_block))[:, :row_block * (span - 1)]  22.6 us
    dot_general x1, matrix products, one_block(): jnp.einsum('qhd,khd->hqk', query_heads, key_heads, preferred_element_type...  14.3 us
    dot_general x1, matrix products, one_block(): jnp.einsum('hqk,khd->qhd', probabilities, value_heads, preferred_element_...  13.8 us
    sub x1, other arithmetic, one_block(): weights = jnp.exp(scores - row_max)  12.1 us
  transfers between devices with their start and end apart: 10, of which 7 were waited for; matrix products, arithmetic and copies ran while one was open for 37% of the time, Pallas kernels for 0%

commit v1 on v0

v1 whole, which is shorter than its diff:
```python
import jax
import jax.numpy as jnp
from jax import lax
from jax.experimental import pallas as pl
from jax.experimental.pallas import tpu as pltpu
from jax.sharding import PartitionSpec as P

PAGE = 128
HEAD_DIM = 64
SPREAD = 384
GROUP = 256
MIB = 1 << 20

epsilon = 1e-06
far_steps = (12, 16, 23, 32, 46, 64, 91)
NEG = float("-inf")


def exchange(block, mask, flip):
    count = lax.axis_size("req")
    pairs = [(r * 2 + t, (r ^ mask) * 2 + (t ^ flip)) for r in range(count) for t in range(2)]
    return lax.ppermute(block, ("req", "tp"), pairs)


def buckets(offsets):
    distance = jnp.abs(offsets)
    far_bucket = 8 + sum((distance >= threshold).astype(jnp.int32) for threshold in far_steps)
    bucket_ids = jnp.where(distance < 8, distance, far_bucket)
    return bucket_ids + jnp.where(offsets > 0, 16, 0).astype(jnp.int32)


def any_spec():
    return pl.BlockSpec(memory_space=pl.ANY)


def smem_spec():
    return pl.BlockSpec(memory_space=pltpu.SMEM)


def params(mib, grid_rank=1):
    return pltpu.CompilerParams(
        dimension_semantics=("arbitrary",) * grid_rank, vmem_limit_bytes=mib * MIB
    )


def lane_order(packing, page_table, arrived, me):
    def body(packing_ref, table_ref, me_ref, rows_ref, *rest):
        row_outs, tag_outs, page_out, sems = rest[:4], rest[4:8], rest[8], rest[9]
        me_here = me_ref[0]
        copies = []
        for m in range(4):
            source = jnp.int32(0)
            pack_slot = jnp.int32(0)
            page = jnp.int32(0)
            page_slot = jnp.int32(0)
            for j in range(4):
                hit = ((packing_ref[j] // 4) ^ me_here) == m
                source = jnp.where(hit, j, source)
                pack_slot = jnp.where(hit, packing_ref[j] % 4, pack_slot)
                owned = ((table_ref[j] // 4) ^ me_here) == m
                page = jnp.where(owned, j, page)
                page_slot = jnp.where(owned, table_ref[j] % 4, page_slot)
            tag_outs[m][0] = pack_slot
            tag_outs[m][1] = page_slot
            page_out[m] = page
            copy = pltpu.make_async_copy(rows_ref.at[source], row_outs[m], sems.at[m])
            copy.start()
            copies.append(copy)
        for copy in copies:
            copy.wait()

    shape = jax.ShapeDtypeStruct(arrived.shape[1:], arrived.dtype)
    outs = pl.pallas_call(
        body,
        grid_spec=pltpu.PrefetchScalarGridSpec(
            num_scalar_prefetch=3,
            grid=(),
            in_specs=[any_spec()],
            out_specs=[any_spec()] * 4 + [smem_spec()] * 5,
            scratch_shapes=[pltpu.SemaphoreType.DMA((4,))],
        ),
        out_shape=[shape] * 4
        + [jax.ShapeDtypeStruct((2,), jnp.int32)] * 4
        + [jax.ShapeDtypeStruct((4,), jnp.int32)],
        name="lane_order",
    )(packing, page_table, me, arrived)
    return outs[:4], outs[4:8], outs[8]


def bias_tiles(rel_bias):
    table = jnp.transpose(rel_bias)
    heads = table.shape[0]

    def body(table_ref, out_ref):
        lane = lax.broadcasted_iota(jnp.int32, (heads, 512), 1)
        bucket_ids = buckets(jnp.where(lane < SPREAD, lane - PAGE, lane - PAGE - 512))
        values = table_ref[...]
        row = jnp.zeros((heads, 512), jnp.float32)
        for b in range(table.shape[1]):
            row = jnp.where(bucket_ids == b, values[:, b : b + 1], row)
        for h in range(heads):
            wide = jnp.broadcast_to(row[h : h + 1, :], (PAGE, 512))
            turned = pltpu.roll(wide, 0, 1, stride=1, stride_axis=0)
            out_ref[h * PAGE : (h + 1) * PAGE, :] = turned[:, :SPREAD]

    return pl.pallas_call(
        body,
        out_shape=jax.ShapeDtypeStruct((heads * PAGE, SPREAD), jnp.float32),
        compiler_params=pltpu.CompilerParams(vmem_limit_bytes=16 * MIB),
        name="bias_tiles",
    )(table)


def normalize(side, first_refs, second_refs, gain_ref, out_ref):
    half = first_refs[0].shape[-1]
    for i, (first_ref, second_ref) in enumerate(zip(first_refs, second_refs)):
        first = first_ref[...].astype(jnp.float32)
        second = second_ref[...].astype(jnp.float32)
        total = jnp.sum(first * first, axis=-1, keepdims=True) + jnp.sum(
            second * second, axis=-1, keepdims=True
        )
        scale = lax.rsqrt(total * (1.0 / (2 * half)) + epsilon)
        left = jnp.where(side == 0, first, second)
        right = jnp.where(side == 0, second, first)
        rows = slice(i * PAGE, (i + 1) * PAGE)
        out_ref[rows, :half] = (left * scale * gain_ref[:, :half]).astype(jnp.bfloat16)
        out_ref[rows, half:] = (right * scale * gain_ref[:, half:]).astype(jnp.bfloat16)


def project(part, first, second, side, gain, weights, earlier):
    half = first[0].shape[1]
    columns = weights[0].shape[1]
    steps = columns // GROUP

    def body(side_ref, f0, f1, s0, s1, gain_ref, wq, wk, wv, *rest):
        q_out, k_out, v_out, own_out, normed = rest[-5:]

        @pl.when(pl.program_id(0) == 0)
        def _():
            normalize(side_ref[0], (f0, f1), (s0, s1), gain_ref, normed)
            own_out[0] = f0[...]
            own_out[1] = f1[...]

        rows = normed[...]
        for w_ref, out in ((wq, q_out), (wk, k_out), (wv, v_out)):
            product = jnp.dot(rows, w_ref[...], preferred_element_type=jnp.float32)
            out[...] = product.astype(jnp.bfloat16).reshape(2, PAGE, GROUP)

    block = pl.BlockSpec((PAGE, half), lambda n, s: (0, 0))
    weight = pl.BlockSpec((2 * half, GROUP), lambda n, s: (0, n))
    out = pl.BlockSpec((2, PAGE, GROUP), lambda n, s: (part, 0, n))
    own = pl.BlockSpec((2, PAGE, half), lambda n, s: (part, 0, 0))
    shape = jax.ShapeDtypeStruct((4, PAGE, columns), jnp.bfloat16)
    return pl.pallas_call(
        body,
        grid_spec=pltpu.PrefetchScalarGridSpec(
            num_scalar_prefetch=1,
            grid=(steps,),
            in_specs=[block] * 4
            + [pl.BlockSpec((1, 2 * half), lambda n, s: (0, 0))]
            + [weight] * 3
            + [any_spec()] * len(earlier),
            out_specs=[out, out, out, own],
            scratch_shapes=[pltpu.VMEM((2 * PAGE, 2 * half), jnp.bfloat16)],
        ),
        out_shape=[shape, shape, shape, jax.ShapeDtypeStruct((4, PAGE, half), jnp.bfloat16)],
        input_output_aliases={9 + i: i for i in range(len(earlier))},
        compiler_params=params(24),
        cost_estimate=pl.CostEstimate(
            flops=2 * 2 * PAGE * 2 * half * 3 * columns,
            transcendentals=0,
            bytes_accessed=3 * 2 * half * columns * 2,
        ),
        name="project",
    )(side, *first, *second, gain, *weights, *earlier)


def lane_of(meta, block):
    lane = jnp.int32(0)
    for m in range(1, 4):
        lane = jnp.where(meta[2 * m] == block, m, lane)
    return lane


def attend(lanes, meta, segments, side, queries, keys_local, values_local, w_out, bias):
    inner = w_out.shape[0]
    width = w_out.shape[1]
    steps = inner // GROUP
    pair = 2 * HEAD_DIM

    def body(meta_ref, seg_ref, side_ref, q_ref, k_ref, v_ref, rows_ref, w_ref, bias_ref,
             own_out, send_out, total, ctx, m_sc, l_sc, a_sc, seg_sc):
        step = pl.program_id(0)

        @pl.when(step == 0)
        def _():
            total[...] = jnp.zeros_like(total)
            for i, m in enumerate(lanes):
                row = rows_ref[pl.ds(meta_ref[8 + m], 1), :]
                seg_sc[i] = jnp.transpose(jnp.broadcast_to(row, (PAGE, PAGE)))

        lane = lax.broadcasted_iota(jnp.int32, (PAGE, pair), 1)
        low = lane < HEAD_DIM
        ones = jnp.ones((PAGE, PAGE), jnp.bfloat16)
        for i, m in enumerate(lanes):
            block = meta_ref[8 + m]
            at = lane_of(meta_ref, block)

            def scores(key_block, key_at, delta, hp):
                cols = slice(hp * pair, (hp + 1) * pair)
                q = q_ref[at, :, cols]
                zero = jnp.zeros_like(q)
                stacked = jnp.concatenate([jnp.where(low, q, zero), jnp.where(low, zero, q)], axis=0)
                s = lax.dot_general(
                    stacked, k_ref[key_at, :, cols], (((1,), (1,)), ((), ())),
                    preferred_element_type=jnp.float32,
                )
                rows = slice(hp * 2 * PAGE, (hp + 1) * 2 * PAGE)
                if delta == 2:
                    s = s + bias_ref[rows, SPREAD - 1 : SPREAD]
                elif delta == -2:
                    s = s + bias_ref[rows, 0:1]
                else:
                    s = s + bias_ref[rows, (delta + 1) * PAGE : (delta + 2) * PAGE]
                same = seg_sc[i] == rows_ref[pl.ds(key_block, 1), :]
                hide = jnp.where(same, 0.0, NEG).astype(jnp.float32)
                return s + jnp.concatenate([hide, hide], axis=0)

            for hp in range(GROUP // pair):
                s = scores(block, at, 0, hp)
                top = jnp.max(s, axis=-1, keepdims=True)
                weights = jnp.exp(s - top).astype(jnp.bfloat16)
                m_sc[hp] = jnp.broadcast_to(top, (2 * PAGE, PAGE))
                l_sc[hp] = jnp.dot(weights, ones, preferred_element_type=jnp.float32)
                a_sc[hp] = jnp.dot(
                    weights, v_ref[at, :, hp * pair : (hp + 1) * pair],
                    preferred_element_type=jnp.float32,
                )

            for delta in (-1, 1, -2, 2):
                key_block = block + delta
                inside = jnp.logical_and(key_block >= 0, key_block < 4)
                if delta > 0:
                    last = block * PAGE + PAGE - 1
                    first = key_block * PAGE
                else:
                    last = key_block * PAGE + PAGE - 1
                    first = block * PAGE
                top_index = 4 * PAGE - 1
                joined = seg_ref[jnp.clip(last, 0, top_index)] == seg_ref[jnp.clip(first, 0, top_index)]

                @pl.when(jnp.logical_and(inside, joined))
                def _(key_block=key_block, delta=delta):
                    key_at = lane_of(meta_ref, key_block)
                    for hp in range(GROUP // pair):
                        s = scores(key_block, key_at, delta, hp)
                        before = m_sc[hp]
                        top = jnp.maximum(before, jnp.max(s, axis=-1, keepdims=True))
                        fade = jnp.exp(before - top)
                        weights = jnp.exp(s - top).astype(jnp.bfloat16)
                        m_sc[hp] = top
                        l_sc[hp] = l_sc[hp] * fade + jnp.dot(
                            weights, ones, preferred_element_type=jnp.float32
                        )
                        a_sc[hp] = a_sc[hp] * fade + jnp.dot(
                            weights, v_ref[key_at, :, hp * pair : (hp + 1) * pair],
                            preferred_element_type=jnp.float32,
                        )

            for hp in range(GROUP // pair):
                mixed = a_sc[hp] / l_sc[hp]
                ctx[i * PAGE : (i + 1) * PAGE, hp * pair : (hp + 1) * pair] = jnp.where(
                    low, mixed[:PAGE], mixed[PAGE:]
                ).astype(jnp.bfloat16)

        total[...] += jnp.dot(ctx[...], w_ref[...], preferred_element_type=jnp.float32)

        @pl.when(step == steps - 1)
        def _():
            half = width // 2
            left = total[:, :half].astype(jnp.bfloat16)
            right = total[:, half:].astype(jnp.bfloat16)
            own_out[...] = jnp.where(side_ref[0] == 0, left, right)
            send_out[...] = jnp.where(side_ref[0] == 0, right, left)

    heads = pl.BlockSpec((4, PAGE, GROUP), lambda g, *_: (0, 0, g))
    out = pl.BlockSpec((2 * PAGE, width // 2), lambda g, *_: (0, 0))
    shape = jax.ShapeDtypeStruct((2 * PAGE, width // 2), jnp.bfloat16)
    rows = GROUP // HEAD_DIM * PAGE
    pairs = GROUP // pair
    return pl.pallas_call(
        body,
        grid_spec=pltpu.PrefetchScalarGridSpec(
            num_scalar_prefetch=3,
            grid=(steps,),
            in_specs=[
                heads,
                heads,
                heads,
                pl.BlockSpec((4, PAGE), lambda g, *_: (0, 0)),
                pl.BlockSpec((GROUP, width), lambda g, *_: (g, 0)),
                pl.BlockSpec((rows, SPREAD), lambda g, *_: (g, 0)),
            ],
            out_specs=[out, out],
            scratch_shapes=[
                pltpu.VMEM((2 * PAGE, width), jnp.float32),
                pltpu.VMEM((2 * PAGE, GROUP), jnp.bfloat16),
                pltpu.VMEM((pairs, 2 * PAGE, PAGE), jnp.float32),
                pltpu.VMEM((pairs, 2 * PAGE, PAGE), jnp.float32),
                pltpu.VMEM((pairs, 2 * PAGE, pair), jnp.float32),
                pltpu.VMEM((2, PAGE, PAGE), jnp.int32),
            ],
        ),
        out_shape=[shape, shape],
        compiler_params=params(24),
        cost_estimate=pl.CostEstimate(
            flops=2 * 2 * PAGE * inner * width * 2,
            transcendentals=2 * PAGE * 512 * 16,
            bytes_accessed=inner * width * 2 + 10 * MIB,
        ),
        name="attend",
    )(meta, segments, side, queries, keys_local, values_local,
      segments.reshape(4, PAGE), w_out, bias)


def residual(lanes, meta, own, received, packed, earlier):
    half = own.shape[1]

    def page(i, meta_ref):
        return jnp.where(i == 0, meta_ref[8 + lanes[0]], meta_ref[8 + lanes[1]])

    def body(meta_ref, own_ref, got_ref, packed_ref, *rest):
        out, first, second = rest[-3:]
        added = own_ref[...].astype(jnp.float32) + got_ref[...].astype(jnp.float32)
        value = (packed_ref[0].astype(jnp.float32) + added).astype(jnp.bfloat16)
        out[0] = value

        @pl.when(pl.program_id(0) == 0)
        def _():
            first[...] = value

        @pl.when(pl.program_id(0) == 1)
        def _():
            second[...] = value

    block = pl.BlockSpec((PAGE, half), lambda i, s: (i, 0))
    alone = pl.BlockSpec((PAGE, half), lambda i, s: (0, 0))
    shape = jax.ShapeDtypeStruct((PAGE, half), jnp.bfloat16)
    return pl.pallas_call(
        body,
        grid_spec=pltpu.PrefetchScalarGridSpec(
            num_scalar_prefetch=1,
            grid=(2,),
            in_specs=[
                block,
                block,
                pl.BlockSpec((1, PAGE, half), lambda i, s: (lane_of(s, page(i, s)), 0, 0)),
            ]
            + [any_spec()] * len(earlier),
            out_specs=[pl.BlockSpec((1, PAGE, half), lambda i, s: (page(i, s), 0, 0)), alone, alone],
        ),
        out_shape=[jax.ShapeDtypeStruct((4, PAGE, half), jnp.bfloat16), shape, shape],
        input_output_aliases={4 + i: i for i in range(len(earlier))},
        compiler_params=params(8),
        name="residual",
    )(meta, own, received, packed, *earlier)


def cross(lanes, meta, side, first, second, gain, cross_key, cross_value, earlier):
    half = first[0].shape[1]
    columns = cross_key.shape[1]
    steps = columns // GROUP

    def body(meta_ref, side_ref, f0, f1, s0, s1, gain_ref, wk, wv, *rest):
        out, final, pages, sems = rest[-4:]
        step = pl.program_id(0)

        @pl.when(step == 0)
        def _():
            normalize(side_ref[0], (f0, f1), (s0, s1), gain_ref, final)

        rows = final[...]
        keys_part = jnp.dot(rows, wk[...], preferred_element_type=jnp.float32).astype(jnp.bfloat16)
        values_part = jnp.dot(rows, wv[...], preferred_element_type=jnp.float32).astype(jnp.bfloat16)
        both = jnp.stack([keys_part, values_part], axis=1)
        here = pl.ds(pl.multiple_of(step * GROUP, GROUP), GROUP)
        pages[0, :, :, here] = both[:PAGE]
        pages[1, :, :, here] = both[PAGE:]

        @pl.when(step == steps - 1)
        def _():
            copies = [
                pltpu.make_async_copy(pages.at[i], out.at[meta_ref[2 * m + 1]], sems.at[i])
                for i, m in enumerate(lanes)
            ]
            for copy in copies:
                copy.start()
            for copy in copies:
                copy.wait()

    block = pl.BlockSpec((PAGE, half), lambda n, *_: (0, 0))
    weight = pl.BlockSpec((2 * half, GROUP), lambda n, *_: (0, n))
    return pl.pallas_call(
        body,
        grid_spec=pltpu.PrefetchScalarGridSpec(
            num_scalar_prefetch=2,
            grid=(steps,),
            in_specs=[block] * 4
            + [pl.BlockSpec((1, 2 * half), lambda n, *_: (0, 0)), weight, weight]
            + [any_spec()] * len(earlier),
            out_specs=any_spec(),
            scratch_shapes=[
                pltpu.VMEM((2 * PAGE, 2 * half), jnp.bfloat16),
                pltpu.VMEM((2, PAGE, 2, columns), jnp.bfloat16),
                pltpu.SemaphoreType.DMA((2,)),
            ],
        ),
        out_shape=jax.ShapeDtypeStruct((4, PAGE, 2, columns), jnp.bfloat16),
        input_output_aliases={9: 0} if earlier else {},
        compiler_params=params(24),
        cost_estimate=pl.CostEstimate(
            flops=2 * 2 * PAGE * 2 * half * 2 * columns,
            transcendentals=0,
            bytes_accessed=2 * 2 * half * columns * 2,
        ),
        name="cross",
    )(meta, side, *first, *second, gain, cross_key, cross_value, *earlier)


def near(rows):
    other_zero = exchange(rows[0], 0, 1)
    own_one = exchange(rows[1], 1, 0)
    other_one = exchange(rows[1], 1, 1)
    return (rows[0], own_one), (other_zero, other_one)


def far(rows):
    other_two = exchange(rows[0], 2, 1)
    other_three = exchange(rows[1], 3, 1)
    own_two = exchange(other_two, 0, 1)
    own_three = exchange(other_three, 0, 1)
    return (own_two, own_three), (other_two, other_three)


def shards(
    arrivals,
    packing,
    segment_ids,
    page_table,
    attn_gain,
    w_query,
    w_key,
    w_value,
    w_out,
    rel_bias,
    final_gain,
    cross_key,
    cross_value,
):
    token_count, half = arrivals.shape
    me = lax.axis_index("req").astype(jnp.int32).reshape(1)
    side = lax.axis_index("tp").astype(jnp.int32).reshape(1)
    rows, tags, pages = lane_order(packing, page_table, arrivals.reshape(4, PAGE, half), me)
    far_own, far_other = far(rows[2:])
    near_own, near_other = near(rows[:2])
    meta = jnp.concatenate([tags[0]] + [exchange(tags[m], m, 0) for m in (1, 2, 3)] + [pages])
    bias = bias_tiles(rel_bias)
    attn_row = attn_gain.reshape(1, 2 * half)
    final_row = final_gain.reshape(1, 2 * half)
    weights = (w_query, w_key, w_value)
    held = project(0, near_own, near_other, side, attn_row, weights, ())
    queries, keys_local, values_local, packed = project(
        1, far_own, far_other, side, attn_row, weights, tuple(held)
    )
    own_far, send_far = attend(
        (2, 3), meta, segment_ids, side, queries, keys_local, values_local, w_out, bias
    )
    got_far = exchange(send_far, 0, 1)
    own_near, send_near = attend(
        (0, 1), meta, segment_ids, side, queries, keys_local, values_local, w_out, bias
    )
    got_near = exchange(send_near, 0, 1)
    hidden, hidden_two, hidden_three = residual((2, 3), meta, own_far, got_far, packed, ())
    far_first, far_second = far((hidden_two, hidden_three))
    hidden, hidden_zero, hidden_one = residual((0, 1), meta, own_near, got_near, packed, (hidden,))
    near_first, near_second = near((hidden_zero, hidden_one))
    cache = cross(
        (0, 1), meta, side, near_first, near_second, final_row, cross_key, cross_value, ()
    )
    cache = cross(
        (2, 3), meta, side, far_first, far_second, final_row, cross_key, cross_value, (cache,)
    )
    return (hidden.reshape(token_count, half), cache)


def solution(mesh):
    return jax.shard_map(
        shards,
        mesh=mesh,
        in_specs=(
            P("req", "tp"),
            P("req"),
            P("req"),
            P("req"),
            P(),
            P(None, "tp"),
            P(None, "tp"),
            P(None, "tp"),
            P("tp", None),
            P(None, "tp"),
            P(),
            P(None, "tp"),
            P(None, "tp"),
        ),
        out_specs=(P("req", "tp"), P("req", None, None, "tp")),
        check_vma=False,
    )
```

time: 413 us -> 147 us (0.36); the launches traced: 408 us -> 147 us
  local copies, waits for them, and re-layouts: 182 us -> 9 us
  Pallas kernels: 0 us -> 82.3 us
  waiting for transfers between devices: 109 us -> 33.7 us
  matrix products: 62.5 us -> 0 us
  other arithmetic: 29.4 us -> 0 us
  between operations: 14.5 us -> 1 us
  starting transfers between devices: 10.3 us -> 20.5 us
    pallas_call x0 -> x10, Pallas kernels: none -> 82.3 us  [the longest x1 34.2 us: lane_order(): pl.pallas_call(body, grid_spec=pltpu.PrefetchScalarGridSpec(num_scalar_pr...]
    psum x1 -> x0, waiting for transfers between devices: 72.7 us -> none  [shards(): summed = lax.psum(product.astype(jnp.bfloat16), 'tp').astype(jnp.float32)]
    dot_general x13 -> x0, matrix products: 62.5 us -> none  [the longest x1 14.3 us: one_block(): jnp.einsum('qhd,khd->hqk', query_heads, key_heads, preferred_element_type...]
    reshape x2 -> x0, local copies, waits for them, and re-layouts: 56.4 us -> none  [the longest x1 51.4 us: offset_tile(): return repeated.reshape(head_count, row_block, span - 1)[:, :, :token_count]]
    unnamed x34 -> x28, local copies, waits for them, and re-layouts: 62.9 us -> 8.25 us
    slice x6 -> x0, local copies, waits for them, and re-layouts: 34.5 us -> none  [the longest x1 22.6 us: offset_tile(): repeated = jnp.tile(bias_row, (1, row_block))[:, :row_block * (span - 1)]]
    another operation x9 -> x0, local copies, waits for them, and re-layouts: 21.8 us -> none  [the longest x2 4.92 us: outgoing(): flat_rows = row_set.reshape(per_device, -1)]
    sub x3 -> x0, other arithmetic: 12.1 us -> none  [the longest x1 12.1 us: one_block(): weights = jnp.exp(scores - row_max)]
  transfers between devices with their start and end apart: 10 -> 19, of which waited for: 7 -> 10; matrix products, arithmetic and copies ran while one was open for 37% -> 1% of each run, Pallas kernels for 0% -> 18%
where the time goes in v1:
time: 147 us
  Pallas kernels  82.3 us (56%)
  waiting for transfers between devices  33.7 us (23%)
  starting transfers between devices  20.5 us (14%)
  local copies, waits for them, and re-layouts  9 us (6%)
    pallas_call x1, Pallas kernels, lane_order(): pl.pallas_call(body, grid_spec=pltpu.PrefetchScalarGridSpec(num_scalar_pr...  34.2 us
    ppermute x19, waiting for transfers between devices, exchange(): return lax.ppermute(block, ('req', 'tp'), pairs)  33.7 us
    ppermute x19, starting transfers between devices, exchange(): return lax.ppermute(block, ('req', 'tp'), pairs)  20.5 us
    pallas_call x2, Pallas kernels, cross(): pl.pallas_call(body, grid_spec=pltpu.PrefetchScalarGridSpec(num_scalar_pr...  15 us
    pallas_call x2, Pallas kernels, attend(): pl.pallas_call(body, grid_spec=pltpu.PrefetchScalarGridSpec(num_scalar_pr...  14.5 us
    pallas_call x2, Pallas kernels, project(): pl.pallas_call(body, grid_spec=pltpu.PrefetchScalarGridSpec(num_scalar_pr...  14.3 us
    unnamed x28, local copies, waits for them, and re-layouts  8.25 us
    pallas_call x2, Pallas kernels, residual(): pl.pallas_call(body, grid_spec=pltpu.PrefetchScalarGridSpec(num_scalar_pr...  3.03 us
  transfers between devices with their start and end apart: 19, of which 10 were waited for; matrix products, arithmetic and copies ran while one was open for 1% of the time, Pallas kernels for 18%

profile of v1, /device:TPU:1, one launch (start us, length us, event | category | flops | bytes accessed | tf_op | source)
XLA Modules:
  0.0 146.6 jit_solution(7686720688819344579)
XLA Ops:
  0.6 34.2 %lane_order.1 = (bf16[128,1024]{1,0:T(8,128)(2,1)}, bf16[128,1024]{1,0:T(8,128)(2,1)}, bf16[128,1024]{1,0:T(8,128)(2,1)}, bf16[128,1024]{1,0:T(8,128)(2,1)}, s32...) custom-call(s32[4]{0:T(128)} %packing_ref.1, s32[4]{0:T(128)} %table_ref.1, s32[1]{0:T(128)} %bitcast.me_ref, ...), custom_call_target="tpu_custom_call" | custom-call | tf_op jit(solution)/shard_map/lane_order/pallas_call | solution.py:73
  34.8 1.5 %collective-permute-start = (s32[2]{0:T(128)}, s32[2]{0:T(128)S(1)}, u32[]{:S(2)}, u32[]{:S(2)}) collective-permute-start(s32[2]{0:T(128)} %get-tuple-element.30), channel_id=1, source_target_pairs={{0,2},{1,3},{2,0},{3,1},{4,6},{5,7},{6,4},{7,5},{8,10},{9,11},{10,... | collective-permute-start | bytes 32 | tf_op jit(solution)/shard_map/ppermute | solution.py:22
  36.3 2.8 %collective-permute-start.1 = (s32[2]{0:T(128)}, s32[2]{0:T(128)S(1)}, u32[]{:S(2)}, u32[]{:S(2)}) collective-permute-start(s32[2]{0:T(128)} %get-tuple-element.31), channel_id=1, source_target_pairs={{0,4},{1,5},{2,6},{3,7},{4,0},{5,1},{6,2},{7,3},{8,12},{9,13},{10,... | collective-permute-start | bytes 32 | tf_op jit(solution)/shard_map/ppermute | solution.py:22
  39.2 0.4 collective-permute-start.2
  39.6 2.6 %collective-permute-start.3 = (bf16[128,1024]{1,0:T(8,128)(2,1)}, bf16[128,1024]{1,0:T(8,128)(2,1)S(1)}, u32[]{:S(2)}, u32[]{:S(2)}) collective-permute-start(bf16[128,1024]{1,0:T(8,128)(2,1)} %get-tuple-element.34), channel_id=1, source_target_pairs={{0,5},{1,4},{2,7},{3,6},{4,1},{5,0},{6,3},{7,2},{8,13},{9,12},{10,... | collective-permute-start | bytes 786440 | tf_op jit(solution)/shard_map/ppermute | solution.py:22
  42.1 0.4 collective-permute-start.5
  42.6 0.1 collective-permute-start.7
  42.6 0.1 collective-permute-start.8
  42.8 1.1 collective-permute-done.2
  43.9 0.9 collective-permute-start.9
  44.7 0.7 copy-done.13
  45.4 1.3 bias_tiles.1.bias_ref
  46.7 0.8 concatenate.3.meta_ref
  47.5 1.3 collective-permute-done.3.s0
  48.8 0.2 collective-permute-start.4
  48.9 5.8 %collective-permute-done.5.s1 = bf16[128,1024]{1,0:T(8,128)(2,1)} collective-permute-done((bf16[128,1024]{1,0:T(8,128)(2,1)}, bf16[128,1024]{1,0:T(8,128)(2,1)}, u32[]{:S(2)}, u32[]{:S(2)}) %collective-permute-start.5) | collective-permute-done | bytes 262176 | tf_op jit(solution)/shard_map/ppermute | solution.py:22
  54.8 0.4 collective-permute-start.6
  55.1 2.4 %collective-permute-done.9.s1 = bf16[128,1024]{1,0:T(8,128)(2,1)} collective-permute-done((bf16[128,1024]{1,0:T(8,128)(2,1)}, bf16[128,1024]{1,0:T(8,128)(2,1)}, u32[]{:S(2)}, u32[]{:S(2)}) %collective-permute-start.9) | collective-permute-done | bytes 262176 | tf_op jit(solution)/shard_map/ppermute | solution.py:22
  57.5 2.2 %copy-done.1 = bf16[2048,1024]{1,0:T(8,128)(2,1)S(1)} copy-done((bf16[2048,1024]{1,0:T(8,128)(2,1)S(1)}, bf16[2048,1024]{1,0:T(8,128)(2,1)}, u32[]{:S(2)}) %copy-start.1) | copy-done | bytes 4194328
  59.7 2.2 %copy-done.3 = bf16[2048,1024]{1,0:T(8,128)(2,1)S(1)} copy-done((bf16[2048,1024]{1,0:T(8,128)(2,1)S(1)}, bf16[2048,1024]{1,0:T(8,128)(2,1)}, u32[]{:S(2)}) %copy-start.3) | copy-done | bytes 4194328
  61.9 2.2 %copy-done.5 = bf16[2048,1024]{1,0:T(8,128)(2,1)S(1)} copy-done((bf16[2048,1024]{1,0:T(8,128)(2,1)S(1)}, bf16[2048,1024]{1,0:T(8,128)(2,1)}, u32[]{:S(2)}) %copy-start.5) | copy-done | bytes 4194328
  64.1 0.9 copy-done.9
  65.0 7.2 %project.2 = (bf16[4,128,1024]{2,1,0:T(8,128)(2,1)S(1)}, bf16[4,128,1024]{2,1,0:T(8,128)(2,1)S(1)}, bf16[4,128,1024]{2,1,0:T(8,128)(2,1)S(1)}, bf16[4,128,1024]{2,1,0:T(8,128)(2,1)S(1)}) custom-call(s32[1]{0:T(128)} %bitcast.2.side_ref, bf16[128,1024]{1,0:T(8,128)(2,1)S(1)} %copy-done.9, bf16[128,1024]{1,0:T(8,128)(2,1)} %collective-permute-done.7.f1, ...), custom_call_target="tpu_custom_call" | custom-call | flops 3221225472 | bytes 12582912 | tf_op jit(solution)/shard_map/project/pallas_call | solution.py:154
  72.3 0.0 copy-start
  72.3 0.0 copy-start.11
  72.4 7.1 %project.3 = (bf16[4,128,1024]{2,1,0:T(8,128)(2,1)S(1)}, bf16[4,128,1024]{2,1,0:T(8,128)(2,1)S(1)}, bf16[4,128,1024]{2,1,0:T(8,128)(2,1)S(1)}, bf16[4,128,1024]{2,1,0:T(8,128)(2,1)S(1)}) custom-call(s32[1]{0:T(128)} %bitcast.2.side_ref, ...), custom_call_target="tpu_custom_call", output_to_operand_aliasing={{0}: (9, {}), {1}: (10, {}), {2}: (11, {}), {3}: (12, {})} | custom-call | flops 3221225472 | bytes 12582912 | tf_op jit(solution)/shard_map/project/pallas_call | solution.py:154
  79.5 7.2 %attend.3 = (bf16[256,1024]{1,0:T(8,128)(2,1)S(1)}, bf16[256,1024]{1,0:T(8,128)(2,1)S(1)}) custom-call(s32[12]{0:T(128)S(1)} %concatenate.3.meta_ref, s32[512]{0:T(512)S(1)} %copy-done.11, s32[1]{0:T(128)} %bitcast.2.side_ref, bf16[4,128,1024]{2,1,0:T(8,128)(2,1)S(1)} %get-tuple-element.42.q_ref, bf16[4,128,1024]{2,1,0:T(8,128)(2,1)S(1)} %get-tuple-element.43.k_ref, ...), custom_call_target="tpu_custom_call" | custom-call | flops 2147483648 | bytes 14680064 | tf_op jit(solution)/shard_map/attend/pallas_call | solution.py:291
  86.7 0.4 collective-permute-start.11
  87.1 7.2 %attend.2 = (bf16[256,1024]{1,0:T(8,128)(2,1)S(1)}, bf16[256,1024]{1,0:T(8,128)(2,1)S(1)}) custom-call(s32[12]{0:T(128)S(1)} %concatenate.3.meta_ref, s32[512]{0:T(512)S(1)} %copy-done.11, s32[1]{0:T(128)} %bitcast.2.side_ref, bf16[4,128,1024]{2,1,0:T(8,128)(2,1)S(1)} %get-tuple-element.42.q_ref, bf16[4,128,1024]{2,1,0:T(8,128)(2,1)S(1)} %get-tuple-element.43.k_ref, ...), custom_call_target="tpu_custom_call" | custom-call | flops 2147483648 | bytes 14680064 | tf_op jit(solution)/shard_map/attend/pallas_call | solution.py:291
  94.4 0.0 copy-start.7
  94.4 1.5 collective-permute-start.10
  95.8 3.8 %collective-permute-done.11.got_ref = bf16[256,1024]{1,0:T(8,128)(2,1)S(1)} collective-permute-done((bf16[256,1024]{1,0:T(8,128)(2,1)S(1)}, bf16[256,1024]{1,0:T(8,128)(2,1)S(1)}, u32[]{:S(2)}, u32[]{:S(2)}) %collective-permute-start.11) | collective-permute-done | bytes 524320 | tf_op jit(solution)/shard_map/ppermute | solution.py:22
  99.7 1.5 %residual.2 = (bf16[4,128,1024]{2,1,0:T(8,128)(2,1)}, bf16[128,1024]{1,0:T(8,128)(2,1)S(1)}, bf16[128,1024]{1,0:T(8,128)(2,1)S(1)}) custom-call(s32[12]{0:T(128)S(1)} %concatenate.3.meta_ref, bf16[256,1024]{1,0:T(8,128)(2,1)S(1)} %get-tuple-element.48.own_ref, bf16[256,1024]{1,0:T(8,128)(2,1)S(1)} %collective-permute-done.11.got_ref, ...), custom_call_target="tpu_custom_call" | custom-call | tf_op jit(solution)/shard_map/residual/pallas_call | solution.py:349
  101.2 3.8 %collective-permute-start.12 = (bf16[128,1024]{1,0:T(8,128)(2,1)S(1)}, bf16[128,1024]{1,0:T(8,128)(2,1)S(1)}, u32[]{:S(2)}, u32[]{:S(2)}) collective-permute-start(bf16[128,1024]{1,0:T(8,128)(2,1)S(1)} %get-tuple-element.52), channel_id=1, source_target_pairs={{0,5},{1,4},{2,7},{3,6},{4,1},{5,0},{6,3},{7,2},{8,13},{9,12},{10,... | collective-permute-start | bytes 786440 | tf_op jit(solution)/shard_map/ppermute | solution.py:22
  105.0 2.0 %collective-permute-start.14 = (bf16[128,1024]{1,0:T(8,128)(2,1)S(1)}, bf16[128,1024]{1,0:T(8,128)(2,1)S(1)}, u32[]{:S(2)}, u32[]{:S(2)}) collective-permute-start(bf16[128,1024]{1,0:T(8,128)(2,1)S(1)} %get-tuple-element.53), channel_id=1, source_target_pairs={{0,7},{1,6},{2,5},{3,4},{4,3},{5,2},{6,1},{7,0},{8,15},{9,14},{10,... | collective-permute-start | bytes 786440 | tf_op jit(solution)/shard_map/ppermute | solution.py:22
  107.0 3.9 %collective-permute-done.10.got_ref = bf16[256,1024]{1,0:T(8,128)(2,1)S(1)} collective-permute-done((bf16[256,1024]{1,0:T(8,128)(2,1)S(1)}, bf16[256,1024]{1,0:T(8,128)(2,1)S(1)}, u32[]{:S(2)}, u32[]{:S(2)}) %collective-permute-start.10) | collective-permute-done | bytes 524320 | tf_op jit(solution)/shard_map/ppermute | solution.py:22
  110.9 1.5 %residual.3 = (bf16[4,128,1024]{2,1,0:T(8,128)(2,1)}, bf16[128,1024]{1,0:T(8,128)(2,1)S(1)}, bf16[128,1024]{1,0:T(8,128)(2,1)S(1)}) custom-call(s32[12]{0:T(128)S(1)} %concatenate.3.meta_ref, bf16[256,1024]{1,0:T(8,128)(2,1)S(1)} %get-tuple-element.45.own_ref, ...), custom_call_target="tpu_custom_call", output_to_operand_aliasing={{0}: (4, {})} | custom-call | tf_op jit(solution)/shard_map/residual/pallas_call | solution.py:349
  112.4 1.7 %collective-permute-start.16 = (bf16[128,1024]{1,0:T(8,128)(2,1)S(1)}, bf16[128,1024]{1,0:T(8,128)(2,1)S(1)}, u32[]{:S(2)}, u32[]{:S(2)}) collective-permute-start(bf16[128,1024]{1,0:T(8,128)(2,1)S(1)} %get-tuple-element.55), channel_id=1, source_target_pairs={{0,2},{1,3},{2,0},{3,1},{4,6},{5,7},{6,4},{7,5},{8,10},{9,11},{10,... | collective-permute-start | bytes 786440 | tf_op jit(solution)/shard_map/ppermute | solution.py:22
  114.1 0.1 collective-permute-start.17
  114.2 1.5 %collective-permute-start.18 = (bf16[128,1024]{1,0:T(8,128)(2,1)S(1)}, bf16[128,1024]{1,0:T(8,128)(2,1)S(1)}, u32[]{:S(2)}, u32[]{:S(2)}) collective-permute-start(bf16[128,1024]{1,0:T(8,128)(2,1)S(1)} %get-tuple-element.55), channel_id=1, source_target_pairs={{0,3},{1,2},{2,1},{3,0},{4,7},{5,6},{6,5},{7,4},{8,11},{9,10},{10,... | collective-permute-start | bytes 786440 | tf_op jit(solution)/shard_map/ppermute | solution.py:22
  115.8 0.1 collective-permute-start.13
  115.8 1.3 collective-permute-done.14.s1
  117.2 0.1 collective-permute-start.15
  117.2 4.8 %collective-permute-done.17.s0 = bf16[128,1024]{1,0:T(8,128)(2,1)S(1)} collective-permute-done((bf16[128,1024]{1,0:T(8,128)(2,1)S(1)}, bf16[128,1024]{1,0:T(8,128)(2,1)S(1)}, u32[]{:S(2)}, u32[]{:S(2)}) %collective-permute-start.17) | collective-permute-done | bytes 262176 | tf_op jit(solution)/shard_map/ppermute | solution.py:22
  122.1 6.1 %collective-permute-done.18.s1 = bf16[128,1024]{1,0:T(8,128)(2,1)S(1)} collective-permute-done((bf16[128,1024]{1,0:T(8,128)(2,1)S(1)}, bf16[128,1024]{1,0:T(8,128)(2,1)S(1)}, u32[]{:S(2)}, u32[]{:S(2)}) %collective-permute-start.18) | collective-permute-done | bytes 262176 | tf_op jit(solution)/shard_map/ppermute | solution.py:22
  128.2 7.5 %cross.2.rest_0_ = bf16[4,128,2,1024]{3,2,1,0:T(2,128)(2,1)} custom-call(s32[12]{0:T(128)S(1)} %concatenate.3.meta_ref, s32[1]{0:T(128)} %bitcast.2.side_ref, bf16[128,1024]{1,0:T(8,128)(2,1)S(1)} %get-tuple-element.54.f0, bf16[128,1024]{1,0:T(8,128)(2,1)S(1)} %collective-permute-done.16.f1, bf16[128,1024]{1,0:T(8,128)(2,1)S(1)} %collective-permute-done.17.s0, ...), custom_call_target="tpu_custom_call" | custom-call | flops 2147483648 | bytes 8388608 | tf_op jit(solution)/shard_map/cross/pallas_call | solution.py:403
  135.7 3.2 %collective-permute-done.15.f1 = bf16[128,1024]{1,0:T(8,128)(2,1)S(1)} collective-permute-done((bf16[128,1024]{1,0:T(8,128)(2,1)S(1)}, bf16[128,1024]{1,0:T(8,128)(2,1)S(1)}, u32[]{:S(2)}, u32[]{:S(2)}) %collective-permute-start.15) | collective-permute-done | bytes 262176 | tf_op jit(solution)/shard_map/ppermute | solution.py:22
  138.9 7.5 %cross.3 = bf16[4,128,2,1024]{3,2,1,0:T(2,128)(2,1)} custom-call(s32[12]{0:T(128)S(1)} %concatenate.3.meta_ref, s32[1]{0:T(128)} %bitcast.2.side_ref, bf16[128,1024]{1,0:T(8,128)(2,1)S(1)} %collective-permute-done.13.f0, bf16[128,1024]{1,0:T(8,128)(2,1)S(1)} %collective-permute-done.15.f1, ...), custom_call_target="tpu_custom_call", output_to_operand_aliasing={{}: (9, {})} | custom-call | flops 2147483648 | bytes 8388608 | tf_op jit(solution)/shard_map/cross/pallas_call | solution.py:403
  (29 shorter events, 0.1 us)
Async XLA Ops:
  0.6 56.9 %copy-start.10 = (f32[2048]{0:T(1024)S(1)}, f32[2048]{0:T(1024)}, u32[]{:S(2)}) copy-start(f32[2048]{0:T(1024)} %param.17) | copy-start | bytes 24580
  34.8 7.7 %collective-permute-start = (s32[2]{0:T(128)}, s32[2]{0:T(128)S(1)}, u32[]{:S(2)}, u32[]{:S(2)}) collective-permute-start(s32[2]{0:T(128)} %get-tuple-element.30), channel_id=1, source_target_pairs={{0,2},{1,3},{2,0},{3,1},{4,6},{5,7},{6,4},{7,5},{8,10},{9,11},{10,... | collective-permute-start | bytes 32 | tf_op jit(solution)/shard_map/ppermute | solution.py:22
  36.3 6.3 %collective-permute-start.1 = (s32[2]{0:T(128)}, s32[2]{0:T(128)S(1)}, u32[]{:S(2)}, u32[]{:S(2)}) collective-permute-start(s32[2]{0:T(128)} %get-tuple-element.31), channel_id=1, source_target_pairs={{0,4},{1,5},{2,6},{3,7},{4,0},{5,1},{6,2},{7,3},{8,12},{9,13},{10,... | collective-permute-start | bytes 32 | tf_op jit(solution)/shard_map/ppermute | solution.py:22
  39.2 4.7 %collective-permute-start.2 = (s32[2]{0:T(128)}, s32[2]{0:T(128)S(1)}, u32[]{:S(2)}, u32[]{:S(2)}) collective-permute-start(s32[2]{0:T(128)} %get-tuple-element.32), channel_id=1, source_target_pairs={{0,6},{1,7},{2,4},{3,5},{4,2},{5,3},{6,0},{7,1},{8,14},{9,15},{10,... | collective-permute-start | bytes 32 | tf_op jit(solution)/shard_map/ppermute | solution.py:22
  39.6 9.2 %collective-permute-start.3 = (bf16[128,1024]{1,0:T(8,128)(2,1)}, bf16[128,1024]{1,0:T(8,128)(2,1)S(1)}, u32[]{:S(2)}, u32[]{:S(2)}) collective-permute-start(bf16[128,1024]{1,0:T(8,128)(2,1)} %get-tuple-element.34), channel_id=1, source_target_pairs={{0,5},{1,4},{2,7},{3,6},{4,1},{5,0},{6,3},{7,2},{8,13},{9,12},{10,... | collective-permute-start | bytes 786440 | tf_op jit(solution)/shard_map/ppermute | solution.py:22
  42.1 12.6 %collective-permute-start.5 = (bf16[128,1024]{1,0:T(8,128)(2,1)}, bf16[128,1024]{1,0:T(8,128)(2,1)}, u32[]{:S(2)}, u32[]{:S(2)}) collective-permute-start(bf16[128,1024]{1,0:T(8,128)(2,1)} %get-tuple-element.35), channel_id=1, source_target_pairs={{0,7},{1,6},{2,5},{3,4},{4,3},{5,2},{6,1},{7,0},{8,15},{9,14},{10,... | collective-permute-start | bytes 786440 | tf_op jit(solution)/shard_map/ppermute | solution.py:22
  42.6 12.6 %collective-permute-start.7 = (bf16[128,1024]{1,0:T(8,128)(2,1)}, bf16[128,1024]{1,0:T(8,128)(2,1)}, u32[]{:S(2)}, u32[]{:S(2)}) collective-permute-start(bf16[128,1024]{1,0:T(8,128)(2,1)} %get-tuple-element.37), channel_id=1, source_target_pairs={{0,2},{1,3},{2,0},{3,1},{4,6},{5,7},{6,4},{7,5},{8,10},{9,11},{10,... | collective-permute-start | bytes 786440 | tf_op jit(solution)/shard_map/ppermute | solution.py:22
  42.6 12.5 %collective-permute-start.8 = (bf16[128,1024]{1,0:T(8,128)(2,1)}, bf16[128,1024]{1,0:T(8,128)(2,1)}, u32[]{:S(2)}, u32[]{:S(2)}) collective-permute-start(bf16[128,1024]{1,0:T(8,128)(2,1)} %get-tuple-element.36.f0), channel_id=1, source_target_pairs={{0,1},{1,0},{2,3},{3,2},{4,5},{5,4},{6,7},{7,6},{8,9},{9,8},{10,11... | collective-permute-start | bytes 786440 | tf_op jit(solution)/shard_map/ppermute | solution.py:22
  43.9 13.6 %collective-permute-start.9 = (bf16[128,1024]{1,0:T(8,128)(2,1)}, bf16[128,1024]{1,0:T(8,128)(2,1)}, u32[]{:S(2)}, u32[]{:S(2)}) collective-permute-start(bf16[128,1024]{1,0:T(8,128)(2,1)} %get-tuple-element.37), channel_id=1, source_target_pairs={{0,3},{1,2},{2,1},{3,0},{4,7},{5,6},{6,5},{7,4},{8,11},{9,10},{10,... | collective-permute-start | bytes 786440 | tf_op jit(solution)/shard_map/ppermute | solution.py:22
  44.7 0.7 copy-start.13
  48.8 23.5 %collective-permute-start.4 = (bf16[128,1024]{1,0:T(8,128)(2,1)S(1)}, bf16[128,1024]{1,0:T(8,128)(2,1)S(1)}, u32[]{:S(2)}, u32[]{:S(2)}) collective-permute-start(bf16[128,1024]{1,0:T(8,128)(2,1)S(1)} %collective-permute-done.3.s0), channel_id=1, source_target_pairs={{0,1},{1,0},{2,3},{3,2},{4,5},{5,4},{6,7},{7,6},{8,9},{9,8},{10,11... | collective-permute-start | bytes 786440 | tf_op jit(solution)/shard_map/ppermute | solution.py:22
  54.8 17.5 %collective-permute-start.6 = (bf16[128,1024]{1,0:T(8,128)(2,1)}, bf16[128,1024]{1,0:T(8,128)(2,1)S(1)}, u32[]{:S(2)}, u32[]{:S(2)}) collective-permute-start(bf16[128,1024]{1,0:T(8,128)(2,1)} %collective-permute-done.5.s1), channel_id=1, source_target_pairs={{0,1},{1,0},{2,3},{3,2},{4,5},{5,4},{6,7},{7,6},{8,9},{9,8},{10,11... | collective-permute-start | bytes 786440 | tf_op jit(solution)/shard_map/ppermute | solution.py:22
  57.5 2.2 %copy-start.1 = (bf16[2048,1024]{1,0:T(8,128)(2,1)S(1)}, bf16[2048,1024]{1,0:T(8,128)(2,1)}, u32[]{:S(2)}) copy-start(bf16[2048,1024]{1,0:T(8,128)(2,1)} %wq.3) | copy-start | bytes 12582916
  59.7 2.2 %copy-start.3 = (bf16[2048,1024]{1,0:T(8,128)(2,1)S(1)}, bf16[2048,1024]{1,0:T(8,128)(2,1)}, u32[]{:S(2)}) copy-start(bf16[2048,1024]{1,0:T(8,128)(2,1)} %wk.5) | copy-start | bytes 12582916
  61.9 2.2 %copy-start.5 = (bf16[2048,1024]{1,0:T(8,128)(2,1)S(1)}, bf16[2048,1024]{1,0:T(8,128)(2,1)}, u32[]{:S(2)}) copy-start(bf16[2048,1024]{1,0:T(8,128)(2,1)} %wv.5) | copy-start | bytes 12582916
  64.1 0.9 copy-start.9
  65.0 7.3 %copy-start.2 = (bf16[2048,1024]{1,0:T(8,128)(2,1)S(1)}, bf16[2048,1024]{1,0:T(8,128)(2,1)}, u32[]{:S(2)}) copy-start(bf16[2048,1024]{1,0:T(8,128)(2,1)} %wq.3) | copy-start | bytes 12582916
  65.0 7.3 %copy-start.4 = (bf16[2048,1024]{1,0:T(8,128)(2,1)S(1)}, bf16[2048,1024]{1,0:T(8,128)(2,1)}, u32[]{:S(2)}) copy-start(bf16[2048,1024]{1,0:T(8,128)(2,1)} %wk.5) | copy-start | bytes 12582916
  65.0 7.3 %copy-start.6 = (bf16[2048,1024]{1,0:T(8,128)(2,1)S(1)}, bf16[2048,1024]{1,0:T(8,128)(2,1)}, u32[]{:S(2)}) copy-start(bf16[2048,1024]{1,0:T(8,128)(2,1)} %wv.5) | copy-start | bytes 12582916
  72.3 7.1 %copy-start = (bf16[1024,2048]{1,0:T(8,128)(2,1)S(1)}, bf16[1024,2048]{1,0:T(8,128)(2,1)}, u32[]{:S(2)}) copy-start(bf16[1024,2048]{1,0:T(8,128)(2,1)} %w_ref.3) | copy-start | bytes 12582916
  72.3 7.1 %copy-start.11 = (s32[512]{0:T(512)S(1)}, s32[512]{0:T(512)}, u32[]{:S(2)}) copy-start(s32[512]{0:T(512)} %seg_ref.3) | copy-start | bytes 6148
  86.7 12.9 %collective-permute-start.11 = (bf16[256,1024]{1,0:T(8,128)(2,1)S(1)}, bf16[256,1024]{1,0:T(8,128)(2,1)S(1)}, u32[]{:S(2)}, u32[]{:S(2)}) collective-permute-start(bf16[256,1024]{1,0:T(8,128)(2,1)S(1)} %get-tuple-element.49), channel_id=1, source_target_pairs={{0,1},{1,0},{2,3},{3,2},{4,5},{5,4},{6,7},{7,6},{8,9},{9,8},{10,11... | collective-permute-start | bytes 1572872 | tf_op jit(solution)/shard_map/ppermute | solution.py:22
  87.1 41.0 %copy-start.8 = (bf16[2048,1024]{1,0:T(8,128)(2,1)S(1)}, bf16[2048,1024]{1,0:T(8,128)(2,1)}, u32[]{:S(2)}) copy-start(bf16[2048,1024]{1,0:T(8,128)(2,1)} %wv.7) | copy-start | bytes 12582916
  94.4 33.8 %copy-start.7 = (bf16[2048,1024]{1,0:T(8,128)(2,1)S(1)}, bf16[2048,1024]{1,0:T(8,128)(2,1)}, u32[]{:S(2)}) copy-start(bf16[2048,1024]{1,0:T(8,128)(2,1)} %wk.7) | copy-start | bytes 12582916
  94.4 33.8 %copy-start.12 = (f32[2048]{0:T(1024)S(1)}, f32[2048]{0:T(1024)}, u32[]{:S(2)}) copy-start(f32[2048]{0:T(1024)} %param.23) | copy-start | bytes 24580
  94.4 16.5 %collective-permute-start.10 = (bf16[256,1024]{1,0:T(8,128)(2,1)S(1)}, bf16[256,1024]{1,0:T(8,128)(2,1)S(1)}, u32[]{:S(2)}, u32[]{:S(2)}) collective-permute-start(bf16[256,1024]{1,0:T(8,128)(2,1)S(1)} %get-tuple-element.46), channel_id=1, source_target_pairs={{0,1},{1,0},{2,3},{3,2},{4,5},{5,4},{6,7},{7,6},{8,9},{9,8},{10,11... | collective-permute-start | bytes 1572872 | tf_op jit(solution)/shard_map/ppermute | solution.py:22
  101.2 14.6 %collective-permute-start.12 = (bf16[128,1024]{1,0:T(8,128)(2,1)S(1)}, bf16[128,1024]{1,0:T(8,128)(2,1)S(1)}, u32[]{:S(2)}, u32[]{:S(2)}) collective-permute-start(bf16[128,1024]{1,0:T(8,128)(2,1)S(1)} %get-tuple-element.52), channel_id=1, source_target_pairs={{0,5},{1,4},{2,7},{3,6},{4,1},{5,0},{6,3},{7,2},{8,13},{9,12},{10,... | collective-permute-start | bytes 786440 | tf_op jit(solution)/shard_map/ppermute | solution.py:22
  105.0 12.2 %collective-permute-start.14 = (bf16[128,1024]{1,0:T(8,128)(2,1)S(1)}, bf16[128,1024]{1,0:T(8,128)(2,1)S(1)}, u32[]{:S(2)}, u32[]{:S(2)}) collective-permute-start(bf16[128,1024]{1,0:T(8,128)(2,1)S(1)} %get-tuple-element.53), channel_id=1, source_target_pairs={{0,7},{1,6},{2,5},{3,4},{4,3},{5,2},{6,1},{7,0},{8,15},{9,14},{10,... | collective-permute-start | bytes 786440 | tf_op jit(solution)/shard_map/ppermute | solution.py:22
  112.4 4.8 %collective-permute-start.16 = (bf16[128,1024]{1,0:T(8,128)(2,1)S(1)}, bf16[128,1024]{1,0:T(8,128)(2,1)S(1)}, u32[]{:S(2)}, u32[]{:S(2)}) collective-permute-start(bf16[128,1024]{1,0:T(8,128)(2,1)S(1)} %get-tuple-element.55), channel_id=1, source_target_pairs={{0,2},{1,3},{2,0},{3,1},{4,6},{5,7},{6,4},{7,5},{8,10},{9,11},{10,... | collective-permute-start | bytes 786440 | tf_op jit(solution)/shard_map/ppermute | solution.py:22
  114.1 7.9 %collective-permute-start.17 = (bf16[128,1024]{1,0:T(8,128)(2,1)S(1)}, bf16[128,1024]{1,0:T(8,128)(2,1)S(1)}, u32[]{:S(2)}, u32[]{:S(2)}) collective-permute-start(bf16[128,1024]{1,0:T(8,128)(2,1)S(1)} %get-tuple-element.54.f0), channel_id=1, source_target_pairs={{0,1},{1,0},{2,3},{3,2},{4,5},{5,4},{6,7},{7,6},{8,9},{9,8},{10,11... | collective-permute-start | bytes 786440 | tf_op jit(solution)/shard_map/ppermute | solution.py:22
  114.2 13.9 %collective-permute-start.18 = (bf16[128,1024]{1,0:T(8,128)(2,1)S(1)}, bf16[128,1024]{1,0:T(8,128)(2,1)S(1)}, u32[]{:S(2)}, u32[]{:S(2)}) collective-permute-start(bf16[128,1024]{1,0:T(8,128)(2,1)S(1)} %get-tuple-element.55), channel_id=1, source_target_pairs={{0,3},{1,2},{2,1},{3,0},{4,7},{5,6},{6,5},{7,4},{8,11},{9,10},{10,... | collective-permute-start | bytes 786440 | tf_op jit(solution)/shard_map/ppermute | solution.py:22
  115.8 19.9 %collective-permute-start.13 = (bf16[128,1024]{1,0:T(8,128)(2,1)S(1)}, bf16[128,1024]{1,0:T(8,128)(2,1)S(1)}, u32[]{:S(2)}, u32[]{:S(2)}) collective-permute-start(bf16[128,1024]{1,0:T(8,128)(2,1)S(1)} %collective-permute-done.12.s0), channel_id=1, source_target_pairs={{0,1},{1,0},{2,3},{3,2},{4,5},{5,4},{6,7},{7,6},{8,9},{9,8},{10,11... | collective-permute-start | bytes 786440 | tf_op jit(solution)/shard_map/ppermute | solution.py:22
  117.2 21.7 %collective-permute-start.15 = (bf16[128,1024]{1,0:T(8,128)(2,1)S(1)}, bf16[128,1024]{1,0:T(8,128)(2,1)S(1)}, u32[]{:S(2)}, u32[]{:S(2)}) collective-permute-start(bf16[128,1024]{1,0:T(8,128)(2,1)S(1)} %collective-permute-done.14.s1), channel_id=1, source_target_pairs={{0,1},{1,0},{2,3},{3,2},{4,5},{5,4},{6,7},{7,6},{8,9},{9,8},{10,11... | collective-permute-start | bytes 786440 | tf_op jit(solution)/shard_map/ppermute | solution.py:22
